TPU v7x, 32 devices: a whole 2x2x4 slice. The times are simulated.
32 devices in a mesh: layer: 4 (over x, core), row: 2 (over y), col: 4 (over z).
Axes of the slice: x: 2, y: 2, z: 4, core: 2. Of those that a mesh axis runs over, the one named last changes fastest.
Arguments:
- schur_window: float32 [4, 2, 256, 2, 4, 256], P(None, 'row', None, None, 'col'), may hold values from -8 to 24, as said below
Outputs:
- factored: float32 [4, 2, 256, 2, 4, 256], P(None, 'row', 'layer', None, 'col')
Inputs may be any that keep to these rules, and one draw needn't show every extreme that they name: `schur_window`: the leading 2048 columns of a symmetric positive definite matrix: its leading 2048 x 2048 block is symmetric and positive definite.
All inputs are finite; a program needn't handle non-finite values.
Results may differ from a plain program's by a relative error of at most 0.0001.
Values sent between devices are 32-bit elements; how exact they have to be, the bound alone decides.
A program may use at most 64 MiB of HBM per device.

v0:
```python
import jax
import jax.numpy as jnp
from jax import lax
from jax.sharding import PartitionSpec as P

PANELS = 2


def spread(array, axis, root):
    mine = lax.axis_index(axis) == root
    return lax.psum(jnp.where(mine, array, jnp.zeros_like(array)), axis)


def solve_rows(factor, column):
    block_count, panel_width, _ = column.shape
    flattened = column.reshape(block_count * panel_width, panel_width)
    solved = jax.scipy.linalg.solve_triangular(factor, flattened.T, lower=True)
    return solved.T.reshape(block_count, panel_width, panel_width)


def shape_panel(factor, solved, row_number, panel_index):
    row_marks = row_number[:, None, None]
    lower_rows = jnp.where(row_marks > panel_index, solved, jnp.zeros_like(solved))
    return jnp.where(row_marks == panel_index, factor[None], lower_rows)


def block_products(row_part, col_part):
    block_count, panel_width, _ = row_part.shape
    slot_count = col_part.shape[0]
    product = jnp.dot(
        row_part.reshape(block_count * panel_width, panel_width),
        col_part.reshape(slot_count * panel_width, panel_width).T,
        precision=lax.Precision.HIGHEST,
        preferred_element_type=jnp.float32,
    )
    return product.reshape(block_count, panel_width, slot_count, panel_width)


def add_slots(updates, row_part, col_part, active):

    def increase(current):
        return current + block_products(row_part, col_part)

    def unchanged(current):
        return current

    return lax.cond(active, increase, unchanged, updates)


def local(schur_window):
    row_blocks = schur_window.shape[0]
    panel_width = schur_window.shape[2]
    col_blocks = schur_window.shape[3]
    held_blocks = schur_window.reshape(row_blocks, panel_width, col_blocks, panel_width)
    grid_rows = lax.axis_size("row")
    grid_cols = lax.axis_size("col")
    layer_count = lax.axis_size("layer")
    layer_here = lax.axis_index("layer")
    col_here = lax.axis_index("col")
    row_number = jnp.arange(row_blocks, dtype=jnp.int32) * grid_rows + lax.axis_index("row")
    col_number = jnp.arange(col_blocks, dtype=jnp.int32) * grid_cols + col_here
    updates = jnp.zeros_like(held_blocks)
    for panel_index in range(PANELS):
        owner_col = panel_index % grid_cols
        owner_slot = panel_index // grid_cols
        pivot_row = panel_index % grid_rows
        pivot_slot = panel_index // grid_rows
        owner_layer = panel_index % layer_count
        column_here = held_blocks[:, :, owner_slot, :]
        if panel_index > 0:
            column_here = column_here - lax.psum(updates[:, :, owner_slot, :], "layer")
        pivot_here = column_here[pivot_slot]
        in_owner_col = col_here == owner_col
        pivot = spread(pivot_here, ("row", "col"), pivot_row * grid_cols + owner_col)
        column = spread(column_here, "col", owner_col)
        factor = jnp.linalg.cholesky(pivot)
        panel_rows = shape_panel(factor, solve_rows(factor, column), row_number, panel_index)
        pieces = []
        for col_slot in range(col_blocks):
            target = col_number[col_slot]
            source_slot = jnp.minimum(target // grid_rows, row_blocks - 1)
            piece = lax.dynamic_index_in_dim(panel_rows, source_slot, 0, keepdims=False)
            pieces.append(spread(piece, "row", target % grid_rows))
        col_panel = jnp.stack(pieces)
        row_part = jnp.where(
            row_number[:, None, None] > panel_index, panel_rows, jnp.zeros_like(panel_rows)
        )
        col_part = jnp.where(
            col_number[:, None, None] > panel_index, col_panel, jnp.zeros_like(col_panel)
        )
        active = layer_here == owner_layer
        updates = add_slots(updates, row_part, col_part, active)
        kept_column = jnp.where(in_owner_col, panel_rows, held_blocks[:, :, owner_slot, :])
        held_blocks = held_blocks.at[:, :, owner_slot, :].set(kept_column)
    summed = lax.psum_scatter(updates, "layer", scatter_dimension=1, tiled=True)
    share_rows = summed.shape[1]
    held_share = lax.dynamic_slice_in_dim(held_blocks, layer_here * share_rows, share_rows, 1)
    factored_cols = (col_number < PANELS)[None, None, :, None]
    upper_part = (row_number[:, None, None, None] < PANELS) & (
        col_number[None, None, :, None] > row_number[:, None, None, None]
    )
    result = jnp.where(factored_cols, held_share, held_share - summed)
    result = jnp.where(upper_part, jnp.zeros_like(result), result)
    return result.reshape(row_blocks, 1, share_rows, col_blocks, 1, panel_width)


def solution(mesh):
    return jax.shard_map(
        local,
        mesh=mesh,
        in_specs=(P(None, "row", None, None, "col", None),),
        out_specs=P(None, "row", "layer", None, "col", None),
        check_vma=False,
    )
```

profile of v0, /device:TPU:0, one launch (start us, length us, event | category | flops | bytes accessed | tf_op | source)
XLA Modules:
  0.0 503.9 jit_solution(17929912383046758080)
XLA Ops:
  6.5 4.6 copy.48
  12.0 1.3 copy.51
  13.4 2.5 copy.52
  21.8 64.0 %all-reduce.13.cloned.1.call-done = f32[256,256]{0,1:T(8,128)} async-done(((f32[256,256]{0,1:T(8,128)}), f32[256,256]{0,1:T(8,128)}) %all-reduce.13.cloned.1.call-update) | async-done | bytes 262160 | tf_op jit(solution)/shard_map/psum | solution.py:11
  87.8 11.7 %cholesky.130 = f32[128,128]{1,0:T(8,128)S(1)} custom-call(f32[128,128]{1,0:T(8,128)S(1)} %cholesky.194), custom_call_target="Cholesky" | custom-call | tf_op jit(solution)/shard_map/jit(cholesky)/cholesky | solution.py:76
  99.6 9.8 %custom-call.13 = f32[1,128,128]{1,2,0:T(8,128)S(1)} custom-call(f32[1,128,128]{2,1,0:T(8,128)S(1)} %get-tuple-element.192), custom_call_target="InvertDiagBlocksLowerTriangular" | custom-call | tf_op jit(solution)/shard_map/jit(cholesky)/cholesky | solution.py:76
  109.9 11.7 %cholesky.147 = f32[128,128]{1,0:T(8,128)S(1)} custom-call(f32[128,128]{1,0:T(8,128)S(1)} %convolution_subtract_fusion.3), custom_call_target="Cholesky" | custom-call | tf_op jit(solution)/shard_map/jit(cholesky)/cholesky | solution.py:76
  123.6 4.3 while.6
  127.9 19.7 %custom-call.14 = f32[2,128,128]{1,2,0:T(8,128)S(1)} custom-call(f32[2,128,128]{2,1,0:T(8,128)S(1)} %get-tuple-element.104), custom_call_target="InvertDiagBlocksLowerTriangular" | custom-call | tf_op jit(solution)/shard_map/jit(_solve_triangular)/triangular_solve | solution.py:17
  147.7 1.7 fusion.16
  149.4 1.6 convolution_subtract_fusion.1
  153.1 1.6 copy.57
  156.8 27.9 %all-reduce.27.cloned.1.call-done = (f32[1,256,256]{1,2,0:T(8,128)}, f32[1,256,256]{1,2,0:T(8,128)}) async-done(((f32[1,256,256]{1,2,0:T(8,128)}, f32[1,256,256]{1,2,0:T(8,128)}), (f32[1,256,256]{1,2,0:T(8,128)}, f32[1,256,256]{1,2,0:T(8,128)})) %all-reduce.27.cloned.1.call-update) | async-done | bytes 524304 | tf_op jit(solution)/shard_map/psum | solution.py:11
  184.7 1.9 pad_maximum_fusion
  189.4 13.5 %conditional.2 = (f32[4,256,2,256]{3,1,2,0:T(8,128)}) conditional(s32[]{:T(128)} %convert_element_type.6, () %tuple.27, (pred[4,256,256]{1,2,0:T(32,128)(4,1)}, s32[2]{0:T(128)S(1)}, f32[4,256,256]{1,2,0:T(8,128)}, f32[4,256,256]{1,2,0:T(8,128)}, f32[2,256,256]{1,2,0:T(8,128)}, /*index=5*/f32[2,256,256]{2,1,0:T(8,128)}, s32[]{:T(128)}) %tuple.110), branch_computations={%region_8.11_spmd, %region_9.12_spmd} | conditional | flops 1611005952 | bytes 11272216 | solution.py:47
  189.4 2.5 copy.59
  191.9 2.6 copy.60
  194.4 2.0 copy.61
  197.8 5.1 %fusion = f32[4,256,2,256]{3,1,2,0:T(8,128)} fusion(pred[4,256,256]{2,1,0:T(32,128)(4,1)S(1)} %copy.58, f32[4,256,256]{2,1,0:T(8,128)} %copy.59, f32[4,256,256]{2,1,0:T(8,128)} %copy.60, f32[2,256,256]{2,1,0:T(8,128)} %copy.61, f32[2,256,256]{2,1,0:T(8,128)} %get-tuple-element.85, pred[2]{0:T(512)(128)(4,1)S(1)} %broadcast_compare_fusion), kind=kOutput, calls=%fused_computation | convolution fusion | flops 1611005952 | bytes 5505026 | tf_op jit(solution)/shard_map/cond/branch_1_fun/dot_general | solution.py:30
  202.9 2.3 slice.129
  205.2 2.6 copy.81
  207.8 35.5 %all-reduce.17.cloned.1.call-done = f32[4,256,256]{1,2,0:T(8,128)} async-done(((f32[4,256,256]{1,2,0:T(8,128)}), f32[4,256,256]{1,2,0:T(8,128)}) %all-reduce.17.cloned.1.call-update) | async-done | bytes 1048592 | tf_op jit(solution)/shard_map/psum | solution.py:71
  243.3 2.5 broadcast_select_fusion
  246.6 1.6 copy.65
  249.8 68.4 %all-reduce.19.cloned.1.call-done = f32[256,256]{0,1:T(8,128)} async-done(((f32[256,256]{0,1:T(8,128)}), f32[256,256]{0,1:T(8,128)}) %all-reduce.19.cloned.1.call-update) | async-done | bytes 262160 | tf_op jit(solution)/shard_map/psum | solution.py:11
  320.3 11.7 %cholesky.164 = f32[128,128]{1,0:T(8,128)S(1)} custom-call(f32[128,128]{1,0:T(8,128)S(1)} %cholesky.197), custom_call_target="Cholesky" | custom-call | tf_op jit(solution)/shard_map/jit(cholesky)/cholesky | solution.py:76
  332.1 9.8 %custom-call.15 = f32[1,128,128]{1,2,0:T(8,128)S(1)} custom-call(f32[1,128,128]{2,1,0:T(8,128)S(1)} %get-tuple-element.188), custom_call_target="InvertDiagBlocksLowerTriangular" | custom-call | tf_op jit(solution)/shard_map/jit(cholesky)/cholesky | solution.py:76
  342.4 11.7 %cholesky.181 = f32[128,128]{1,0:T(8,128)S(1)} custom-call(f32[128,128]{1,0:T(8,128)S(1)} %convolution_subtract_fusion.2), custom_call_target="Cholesky" | custom-call | tf_op jit(solution)/shard_map/jit(cholesky)/cholesky | solution.py:76
  356.9 4.3 while.7
  357.7 1.4 bitcast_dynamic-update-slice_fusion.5
  359.7 1.4 bitcast_dynamic-update-slice_fusion.5
  361.2 19.7 %custom-call.16 = f32[2,128,128]{1,2,0:T(8,128)S(1)} custom-call(f32[2,128,128]{2,1,0:T(8,128)S(1)} %get-tuple-element.105), custom_call_target="InvertDiagBlocksLowerTriangular" | custom-call | tf_op jit(solution)/shard_map/jit(_solve_triangular)/triangular_solve | solution.py:17
  381.7 1.7 fusion.14
  383.4 1.6 convolution_subtract_fusion
  386.7 1.6 copy.67
  388.3 1.3 copy.71
  389.6 1.4 select_select_fusion
  392.3 1.3 copy.114
  394.8 25.5 %all-reduce.25.cloned.1.call-done = (f32[1,256,256]{1,2,0:T(8,128)}, f32[1,256,256]{1,2,0:T(8,128)}) async-done(((f32[1,256,256]{1,2,0:T(8,128)}, f32[1,256,256]{1,2,0:T(8,128)}), (f32[1,256,256]{1,2,0:T(8,128)}, f32[1,256,256]{1,2,0:T(8,128)})) %all-reduce.25.cloned.1.call-update) | async-done | bytes 524304 | tf_op jit(solution)/shard_map/psum | solution.py:11
  420.3 1.9 pad_maximum_fusion.1
  423.0 4.3 copy.76
  429.8 2.8 constant_dynamic-update-slice_fusion.2
  432.6 1.3 copy.68
  434.0 2.9 select_dynamic-update-slice_fusion
  436.9 53.2 %all-reduce.23.cloned.1.call-done = f32[4,256,2,256]{3,0,2,1:T(4,128)} async-done(((f32[4,256,2,256]{3,0,2,1:T(4,128)}), f32[4,256,2,256]{3,0,2,1:T(4,128)}) %all-reduce.23.cloned.1.call-update) | async-done | bytes 2097168
  490.1 1.9 constant_dynamic-slice_fusion.2
  492.0 1.4 copy.77
  494.7 2.1 copy.78
  (102 shorter events, 33.7 us)
Async XLA Ops:
  6.5 79.2 %all-reduce.13.cloned.1.call-start = ((), (), s32[]{:S(2)}) async-start(), calls=%async_computation | async-start | bytes 524288 | tf_op jit(solution)/shard_map/psum | solution.py:11
  11.9 135.9 %all-reduce.15.cloned.1.call-start = ((), (), s32[]{:S(2)}) async-start(), calls=%async_computation.1 | async-start | bytes 2097152 | tf_op jit(solution)/shard_map/psum | solution.py:11
  15.9 168.8 %all-reduce.27.cloned.1.call-start = ((), (), s32[]{:S(2)}) async-start(), calls=%async_computation.7 | async-start | bytes 1048576 | tf_op jit(solution)/shard_map/psum | solution.py:11
  154.9 1.0 copy-start.6
  156.7 86.6 %all-reduce.17.cloned.1.call-start = ((), (), s32[]{:S(2)}) async-start(), calls=%async_computation.2 | async-start | bytes 2097152 | tf_op jit(solution)/shard_map/psum | solution.py:71
  207.8 110.4 %all-reduce.19.cloned.1.call-start = ((), (), s32[]{:S(2)}) async-start(), calls=%async_computation.3 | async-start | bytes 524288 | tf_op jit(solution)/shard_map/psum | solution.py:11
  246.6 135.1 %all-reduce.21.cloned.1.call-start = ((), (), s32[]{:S(2)}) async-start(), calls=%async_computation.4 | async-start | bytes 2097152 | tf_op jit(solution)/shard_map/psum | solution.py:11
  249.5 170.7 %all-reduce.25.cloned.1.call-start = ((), (), s32[]{:S(2)}) async-start(), calls=%async_computation.6 | async-start | bytes 1048576 | tf_op jit(solution)/shard_map/psum | solution.py:11
  388.3 2.8 copy-start.2
  391.1 1.1 copy-start.5
  392.3 1.4 copy-start.8
  392.3 30.7 %copy-start.1 = (f32[4,256,256]{1,2,0:T(8,128)S(1)}, f32[4,256,256]{1,2,0:T(8,128)}, u32[]{:S(2)}) copy-start(f32[4,256,256]{1,2,0:T(8,128)} %broadcast.368) | copy-start | bytes 3145732
  392.3 97.8 %all-reduce.23.cloned.1.call-start = ((), (), s32[]{:S(2)}) async-start(), calls=%async_computation.5 | async-start | bytes 4194304
  427.2 1.2 copy-start
  429.8 2.8 copy-start.3
  436.9 56.5 %copy-start.4 = (f32[4,256,2,256]{1,3,0,2:T(8,128)S(1)}, f32[4,256,2,256]{1,3,0,2:T(8,128)}, u32[]{:S(2)}) copy-start(f32[4,256,2,256]{1,3,0,2:T(8,128)} %select_dynamic-update-slice_fusion) | copy-start | bytes 6291460
Sparse Core Ops, SparseCore 0:
  12.0 73.7 all-reduce.12
  88.1 51.2 all-reduce.14
  156.8 27.8 all-reduce.26
  207.9 35.3 all-reduce.16
  246.7 71.4 all-reduce.18
  320.4 51.2 all-reduce.20
  392.4 27.8 all-reduce.24
  427.4 62.6 all-reduce.22
where the time goes:
time: 513 us; the launch traced here: 504 us
  waiting for transfers between devices  275 us (54%)
  other arithmetic  130 us (25%)
  local copies, waits for them, and re-layouts  62.2 us (12%)
  between operations  22.3 us (4%)
  matrix products  13.9 us (3%)
    psum x6, waiting for transfers between devices, spread(): return lax.psum(jnp.where(mine, array, jnp.zeros_like(array)), axis)  186 us
    another operation x13, other arithmetic, local(): factor = jnp.linalg.cholesky(pivot)  68.6 us
    unnamed x9, waiting for transfers between devices  53.4 us
    another operation x5, other arithmetic, solve_rows(): solved = jax.scipy.linalg.solve_triangular(factor, flattened.T, lower=True)  39.4 us
    psum x1, waiting for transfers between devices, local(): column_here = column_here - lax.psum(updates[:, :, owner_slot, :], 'layer')  35.5 us
    unnamed x21, local copies, waits for them, and re-layouts  13.2 us
    another operation x6, local copies, waits for them, and re-layouts  10.3 us
  transfers between devices with their start and end apart: 8, of which 6 were waited for; matrix products, arithmetic and copies ran while one was open for 28% of the time, Pallas kernels for 0%

commit v1 on v0

v1 whole, which is shorter than its diff:
```python
import functools

import jax
import jax.numpy as jnp
from jax import lax
from jax.experimental import pallas as pl
from jax.experimental.pallas import tpu as pltpu
from jax.sharding import PartitionSpec as P

PANELS = 2
GROUP = 8
BLOCKS = ((0, 0), (1, 0), (1, 1))


def dot(a, b, lhs, rhs):
    return lax.dot_general(
        a, b, (((lhs,), (rhs,)), ((), ())),
        precision=lax.Precision.HIGHEST, preferred_element_type=jnp.float32,
    )


def matmul(a, b):
    return dot(a, b, 1, 0)


def matmul_t(a, b):
    return dot(a, b, 1, 1)


def eliminate(aug, half):
    lane = lax.broadcasted_iota(jnp.int32, (GROUP, half), 1)
    sub = lax.broadcasted_iota(jnp.int32, (GROUP, 2 * half), 0)

    def step(s, carry):
        first = pl.multiple_of(s * GROUP, GROUP)
        block = aug[pl.ds(first, GROUP), :]
        turned = pltpu.roll(block[:, :half], lax.rem(half - first, half), 1)
        rows = [jnp.broadcast_to(block[j : j + 1, :], (GROUP, 2 * half)) for j in range(GROUP)]
        entry = [
            [jnp.broadcast_to(turned[j : j + 1, k : k + 1], (GROUP, half)) if k >= j else None for k in range(GROUP)]
            for j in range(GROUP)
        ]
        done = jnp.zeros((GROUP, 2 * half), jnp.float32)
        for j in range(GROUP):
            scale = lax.rsqrt(entry[j][j])
            row = rows[j] * jnp.concatenate([scale, scale], axis=1)
            done = jnp.where(sub == j, row, done)
            low = [entry[j][k] * scale if k > j else None for k in range(GROUP)]
            for k in range(j + 1, GROUP):
                for m in range(k, GROUP):
                    entry[k][m] = entry[k][m] - low[k] * low[m]
                rows[k] = rows[k] - jnp.concatenate([low[k], low[k]], axis=1) * row
        later = jnp.where(lane >= first + GROUP, done[:, :half], 0.0)
        aug[...] -= dot(later, done, 0, 0)
        aug[pl.ds(first, GROUP), :] = done
        return carry

    lax.fori_loop(0, half // GROUP, step, 0)


def factor_panel(block, aug, factor, inverse, width):
    half = width // 2
    row = lax.broadcasted_iota(jnp.int32, (half, half), 0)
    col = lax.broadcasted_iota(jnp.int32, (half, half), 1)
    eye = jnp.where(row == col, 1.0, 0.0).astype(jnp.float32)
    zero = jnp.zeros((half, half), jnp.float32)

    def diagonal(value):
        aug[:, :half] = value
        aug[:, half:] = eye
        eliminate(aug, half)
        return jnp.where(row <= col, aug[:, :half], 0.0).T, aug[:, half:]

    low1, inv1 = diagonal(block[:half, :half])
    factor[:half, :half] = low1
    inverse[:half, :half] = inv1
    factor[:half, half:] = zero
    inverse[:half, half:] = zero
    below = matmul_t(block[half:, :half], inv1)
    factor[half:, :half] = below
    low2, inv2 = diagonal(block[half:, half:] - matmul_t(below, below))
    factor[half:, half:] = low2
    inverse[half:, half:] = inv2
    inverse[half:, :half] = -matmul(inv2, matmul(below, inverse[:half, :half]))


def kernel(
    sizes, top, share, out, diag, across, panel, aug, factor, inverse, cross, rest, left,
    diag_send, diag_recv, pass_send, pass_recv, across_send, across_recv, panel_send, panel_recv, local_sem,
):
    layers, grid_rows, grid_cols, row_blocks, col_blocks, width = sizes
    rows_here = width // layers
    me_layer, me_row, me_col = lax.axis_index("layer"), lax.axis_index("row"), lax.axis_index("col")

    def at(layer, row, col):
        return (lax.rem(me_layer + layer, layers), lax.rem(me_row + row, grid_rows), lax.rem(me_col + col, grid_cols))

    def remote(src, dst, send, recv, target):
        return pltpu.make_async_remote_copy(
            src_ref=src, dst_ref=dst, send_sem=send, recv_sem=recv, device_id=target,
            device_id_type=pl.DeviceIdType.MESH,
        )

    grid_peers = [(row, col) for row in range(grid_rows) for col in range(grid_cols) if row or col]
    barrier = pltpu.get_barrier_semaphore()
    for row, col in grid_peers:
        pl.semaphore_signal(barrier, inc=1, device_id=at(0, row, col), device_id_type=pl.DeviceIdType.MESH)
    for layer in range(1, layers):
        pl.semaphore_signal(barrier, inc=1, device_id=at(layer, 0, 0), device_id_type=pl.DeviceIdType.MESH)
    pl.semaphore_wait(barrier, len(grid_peers) + layers - 1)

    def stripe(layer):
        return pl.ds(pl.multiple_of(layer * rows_here, rows_here), rows_here)

    def diag_copy(b, n):
        src = top.at[stripe(me_layer), pl.ds(0, width)]
        dst = diag.at[b, stripe(me_layer), :]
        return remote(src, dst, diag_send.at[b, n], diag_recv.at[b], at(0, *grid_peers[n]))

    def diag_local(b):
        return pltpu.make_async_copy(
            top.at[stripe(me_layer), pl.ds(0, width)], diag.at[b, stripe(me_layer), :], local_sem.at[b]
        )

    def pass_copy(b, n):
        part = diag.at[b, stripe(me_layer), :]
        return remote(part, part, pass_send.at[b, n - 1], pass_recv.at[b, n - 1], at(n, 0, 0))

    def across_copy(k, n):
        return remote(top, across.at[k], across_send.at[k, n - 1], across_recv.at[k], at(0, n, 0))

    def across_local(k):
        return pltpu.make_async_copy(top, across.at[k], local_sem.at[len(BLOCKS) + k])

    def panel_copy(k, n):
        return remote(share.at[:, pl.ds(0, width)], panel.at[k], panel_send.at[k, n - 1], panel_recv.at[k], at(0, 0, n))

    def panel_local(k):
        return pltpu.make_async_copy(
            share.at[:, pl.ds(0, width)], panel.at[k], local_sem.at[len(BLOCKS) + PANELS + k]
        )

    owners = [(me_row == i) & (me_col == j) for i, j in BLOCKS]
    for b in range(len(BLOCKS)):

        @pl.when(owners[b])
        def _(b=b):
            for n in range(len(grid_peers)):
                diag_copy(b, n).start()
            diag_local(b).start()

    for k in range(PANELS):

        @pl.when(me_col == k)
        def _(k=k):
            for n in range(1, grid_cols):
                panel_copy(k, n).start()
            panel_local(k).start()

        @pl.when(me_row == k)
        def _(k=k):
            for n in range(1, grid_rows):
                across_copy(k, n).start()
            across_local(k).start()

    for b in range(len(BLOCKS)):

        @pl.when(owners[b])
        def _(b=b):
            diag_local(b).wait()

        @pl.when(jnp.logical_not(owners[b]))
        def _(b=b):
            diag_copy(b, 0).wait_recv()

        for n in range(1, layers):
            pass_copy(b, n).start()

    def diag_arrived(b):
        for n in range(1, layers):
            pass_copy(b, n).wait_recv()

    diag_arrived(0)
    factor_panel(diag.at[0], aug, factor.at[0], inverse.at[0], width)
    diag_arrived(1)
    cross[...] = matmul_t(diag[1], inverse[0])
    diag_arrived(2)
    rest[...] = diag[2] - matmul_t(cross[...], cross[...])
    factor_panel(rest, aug, factor.at[1], inverse.at[1], width)

    for k in range(PANELS):

        @pl.when(me_col == k)
        def _(k=k):
            panel_local(k).wait()

        @pl.when(me_col != k)
        def _(k=k):
            panel_copy(k, 1).wait_recv()

        @pl.when(me_row == k)
        def _(k=k):
            across_local(k).wait()

        @pl.when(me_row != k)
        def _(k=k):
            across_copy(k, 1).wait_recv()

    left[0] = matmul_t(panel[0], inverse[0])
    left[1] = matmul_t(panel[1] - matmul_t(left[0], cross[...]), inverse[1])
    right0 = matmul(inverse[0], across[0])
    right1 = matmul(inverse[1], across[1] - matmul(cross[...], right0))
    here = stripe(me_layer)
    first0 = jnp.where(me_row == 0, factor[0, here, :], left[0, :rows_here, :])
    first1 = jnp.where(me_row == 0, 0.0, jnp.where(me_row == 1, factor[1, here, :], left[1, :rows_here, :]))
    updated = share[...] - matmul(left[0], right0) - matmul(left[1], right1)
    for slot in range(col_blocks):
        number = slot * grid_cols + me_col
        columns = slice(slot * width, (slot + 1) * width)
        out[:, columns] = jnp.where(number == 0, left[0], jnp.where(number == 1, left[1], updated[:, columns]))
        plain = jnp.where(me_row < PANELS, 0.0, updated[:rows_here, columns])
        out[:rows_here, columns] = jnp.where(number == 0, first0, jnp.where(number == 1, first1, plain))

    for b in range(len(BLOCKS)):

        @pl.when(owners[b])
        def _(b=b):
            for n in range(len(grid_peers)):
                diag_copy(b, n).wait_send()

        for n in range(1, layers):
            pass_copy(b, n).wait_send()
    for k in range(PANELS):

        @pl.when(me_col == k)
        def _(k=k):
            for n in range(1, grid_cols):
                panel_copy(k, n).wait_send()

        @pl.when(me_row == k)
        def _(k=k):
            for n in range(1, grid_rows):
                across_copy(k, n).wait_send()


def local(sizes, schur_window):
    layers, grid_rows, grid_cols, row_blocks, col_blocks, width = sizes
    rows_here = width // layers
    held = schur_window.reshape(row_blocks, width, col_blocks * width)
    share = lax.dynamic_slice_in_dim(held, lax.axis_index("layer") * rows_here, rows_here, 1)
    share = share.reshape(row_blocks * rows_here, col_blocks * width)
    top = held[0]
    vmem = pl.BlockSpec(memory_space=pltpu.VMEM)
    dma = pltpu.SemaphoreType.DMA
    diagonals, peers, half = len(BLOCKS), grid_rows * grid_cols - 1, width // 2
    f32 = jnp.float32
    result = pl.pallas_call(
        functools.partial(kernel, sizes),
        out_shape=jax.ShapeDtypeStruct(share.shape, f32),
        in_specs=[vmem, vmem],
        out_specs=vmem,
        scratch_shapes=[
            pltpu.VMEM((diagonals, width, width), f32),
            pltpu.VMEM((PANELS, width, col_blocks * width), f32),
            pltpu.VMEM((PANELS, row_blocks * rows_here, width), f32),
            pltpu.VMEM((half, width), f32),
            pltpu.VMEM((PANELS, width, width), f32),
            pltpu.VMEM((PANELS, width, width), f32),
            pltpu.VMEM((width, width), f32),
            pltpu.VMEM((width, width), f32),
            pltpu.VMEM((PANELS, row_blocks * rows_here, width), f32),
            dma((diagonals, peers)),
            dma((diagonals,)),
            dma((diagonals, layers - 1)),
            dma((diagonals, layers - 1)),
            dma((PANELS, grid_rows - 1)),
            dma((PANELS,)),
            dma((PANELS, grid_cols - 1)),
            dma((PANELS,)),
            dma((diagonals + 2 * PANELS,)),
        ],
        compiler_params=pltpu.CompilerParams(collective_id=0, has_side_effects=True),
        name="window",
    )(top, share)
    return result.reshape(row_blocks, 1, rows_here, col_blocks, 1, width)


def solution(mesh):
    def body(schur_window):
        row_blocks, _, width, col_blocks, _, _ = schur_window.shape
        sizes = (mesh.shape["layer"], mesh.shape["row"], mesh.shape["col"], row_blocks, col_blocks, width)
        return local(sizes, schur_window)

    return jax.shard_map(
        body,
        mesh=mesh,
        in_specs=(P(None, "row", None, None, "col", None),),
        out_specs=P(None, "row", "layer", None, "col", None),
        check_vma=False,
    )
```

time: 513 us -> 84.1 us (0.16)
  the two profiles are of different devices: /device:TPU:0 before, /device:TPU:29 now
where the time goes in v1:
time: 84.1 us; the launch traced here: 83.8 us
  Pallas kernels  65.5 us (78%)
  local copies, waits for them, and re-layouts  10.6 us (13%)
  other arithmetic  7.7 us (9%)
    pallas_call x1, Pallas kernels, local(): pl.pallas_call(functools.partial(kernel, sizes), out_shape=jax.ShapeDtype...  65.5 us
    unnamed x1, other arithmetic  7.7 us
    reshape x1, local copies, waits for them, and re-layouts, local(): held = schur_window.reshape(row_blocks, width, col_blocks * width)  2.74 us
    slice x1, local copies, waits for them, and re-layouts, local(): top = held[0]  2.68 us
    reshape x1, local copies, waits for them, and re-layouts, local(): return result.reshape(row_blocks, 1, rows_here, col_blocks, 1, width)  2.45 us
    dynamic_slice x1, local copies, waits for them, and re-layouts, local(): lax.dynamic_slice_in_dim(held, lax.axis_index('layer') * rows_here, rows_...  1.87 us

profile of v1, /device:TPU:29, one launch (start us, length us, event | category | flops | bytes accessed | tf_op | source)
XLA Modules:
  0.0 83.8 jit_solution(9591904579263707337)
XLA Ops:
  0.0 7.7 %reduce.1 = f32[4,256,2,256]{3,2,1,0:T(2,128)S(1)} reduce(f32[4,1,256,2,1,256]{5,4,3,2,1,0:T(1,128)} %param.1, f32[]{:T(128)} %constant.12), dimensions={1,4}, to_apply=%param.1.reduce_sub_computation | reduce | bytes 4194308 | tf_op args[0]
  7.7 2.7 %reshape.11 = f32[4,256,512]{2,1,0:T(8,128)} reshape(f32[4,256,2,256]{3,2,1,0:T(2,128)S(1)} %reduce.1) | data formatting | bytes 4194304 | tf_op jit(solution)/shard_map/reshape | solution.py:249
  10.4 1.9 %constant_dynamic-slice_fusion = f32[4,64,512]{2,1,0:T(8,128)} fusion(f32[4,256,512]{2,1,0:T(8,128)} %reshape.11, s32[]{:T(128)S(6)} %select_n.3), kind=kLoop, calls=%fused_computation.1 | loop fusion | bytes 1048580 | tf_op jit(solution)/shard_map/dynamic_slice | solution.py:250
  12.3 2.7 %slice_reduce_fusion = f32[256,2,256]{2,1,0:T(2,128)S(1)} fusion(f32[4,1,256,2,1,256]{5,4,3,2,1,0:T(1,128)} %param.1), kind=kLoop, calls=%fused_computation | loop fusion | bytes 1048576 | tf_op jit(solution)/shard_map/slice | solution.py:252
  15.0 0.8 copy.3
  15.8 65.5 %window.1 = f32[256,512]{1,0:T(8,128)} custom-call(f32[256,512]{1,0:T(8,128)} %bitcast.3, f32[256,512]{1,0:T(8,128)} %bitcast.4), custom_call_target="tpu_custom_call" | custom-call | tf_op jit(solution)/shard_map/window/pallas_call | solution.py:257
  81.4 2.5 %reshape.14 = f32[4,1,64,2,1,256]{5,4,3,2,1,0:T(1,128)} reshape(f32[256,512]{1,0:T(8,128)} %window.1) | data formatting | bytes 1048576 | tf_op jit(solution)/shard_map/reshape | solution.py:285

commit v2 on v1

--- a/solution.py
+++ b/solution.py
@@ -85,8 +85,8 @@
 
 
 def kernel(
-    sizes, top, share, out, diag, across, panel, aug, factor, inverse, cross, rest, left,
-    diag_send, diag_recv, pass_send, pass_recv, across_send, across_recv, panel_send, panel_recv, local_sem,
+    sizes, window, out, diag, across, panel, share, staged, aug, factor, inverse, cross, rest, left,
+    diag_send, diag_recv, pass_send, pass_recv, across_send, across_recv, panel_send, panel_recv, local_sem, share_sem, out_sem,
 ):
     layers, grid_rows, grid_cols, row_blocks, col_blocks, width = sizes
     rows_here = width // layers
@@ -100,6 +100,14 @@
             src_ref=src, dst_ref=dst, send_sem=send, recv_sem=recv, device_id=target,
             device_id_type=pl.DeviceIdType.MESH,
         )
+
+    def stripe(layer):
+        return pl.ds(pl.multiple_of(layer * rows_here, rows_here), rows_here)
+
+    here = stripe(me_layer)
+
+    def share_copy(slot):
+        return pltpu.make_async_copy(window.at[:, 0, here, slot, 0, :], share.at[slot], share_sem.at[slot])
 
     grid_peers = [(row, col) for row in range(grid_rows) for col in range(grid_cols) if row or col]
     barrier = pltpu.get_barrier_semaphore()
@@ -107,38 +115,38 @@
         pl.semaphore_signal(barrier, inc=1, device_id=at(0, row, col), device_id_type=pl.DeviceIdType.MESH)
     for layer in range(1, layers):
         pl.semaphore_signal(barrier, inc=1, device_id=at(layer, 0, 0), device_id_type=pl.DeviceIdType.MESH)
+    for slot in range(col_blocks):
+        share_copy(slot).start()
     pl.semaphore_wait(barrier, len(grid_peers) + layers - 1)
 
-    def stripe(layer):
-        return pl.ds(pl.multiple_of(layer * rows_here, rows_here), rows_here)
+    diag_src = window.at[0, 0, here, 0, 0, :]
 
     def diag_copy(b, n):
-        src = top.at[stripe(me_layer), pl.ds(0, width)]
-        dst = diag.at[b, stripe(me_layer), :]
-        return remote(src, dst, diag_send.at[b, n], diag_recv.at[b], at(0, *grid_peers[n]))
+        return remote(diag_src, diag.at[b, here, :], diag_send.at[b, n], diag_recv.at[b], at(0, *grid_peers[n]))
 
     def diag_local(b):
-        return pltpu.make_async_copy(
-            top.at[stripe(me_layer), pl.ds(0, width)], diag.at[b, stripe(me_layer), :], local_sem.at[b]
+        return pltpu.make_async_copy(diag_src, diag.at[b, here, :], local_sem.at[b])
+
+    def pass_copy(b, n):
+        part = diag.at[b, here, :]
+        return remote(part, part, pass_send.at[b, n - 1], pass_recv.at[b, n - 1], at(n, 0, 0))
+
+    def across_copy(k, slot, n):
+        return remote(
+            window.at[0, 0, :, slot, 0, :], across.at[k, slot], across_send.at[k, slot, n - 1],
+            across_recv.at[k, slot], at(0, n, 0),
         )
 
-    def pass_copy(b, n):
-        part = diag.at[b, stripe(me_layer), :]
-        return remote(part, part, pass_send.at[b, n - 1], pass_recv.at[b, n - 1], at(n, 0, 0))
-
-    def across_copy(k, n):
-        return remote(top, across.at[k], across_send.at[k, n - 1], across_recv.at[k], at(0, n, 0))
-
-    def across_local(k):
-        return pltpu.make_async_copy(top, across.at[k], local_sem.at[len(BLOCKS) + k])
+    def across_local(k, slot):
+        return pltpu.make_async_copy(window.at[0, 0, :, slot, 0, :], across.at[k, slot], across_recv.at[k, slot])
+
+    panel_src = window.at[:, 0, here, 0, 0, :]
 
     def panel_copy(k, n):
-        return remote(share.at[:, pl.ds(0, width)], panel.at[k], panel_send.at[k, n - 1], panel_recv.at[k], at(0, 0, n))
+        return remote(panel_src, panel.at[k], panel_send.at[k, n - 1], panel_recv.at[k], at(0, 0, n))
 
     def panel_local(k):
-        return pltpu.make_async_copy(
-            share.at[:, pl.ds(0, width)], panel.at[k], local_sem.at[len(BLOCKS) + PANELS + k]
-        )
+        return pltpu.make_async_copy(panel_src, panel.at[k], panel_recv.at[k])
 
     owners = [(me_row == i) & (me_col == j) for i, j in BLOCKS]
     for b in range(len(BLOCKS)):
@@ -159,9 +167,10 @@
 
         @pl.when(me_row == k)
         def _(k=k):
-            for n in range(1, grid_rows):
-                across_copy(k, n).start()
-            across_local(k).start()
+            for slot in range(col_blocks):
+                for n in range(1, grid_rows):
+                    across_copy(k, slot, n).start()
+                across_local(k, slot).start()
 
     for b in range(len(BLOCKS)):
 
@@ -188,38 +197,48 @@
     rest[...] = diag[2] - matmul_t(cross[...], cross[...])
     factor_panel(rest, aug, factor.at[1], inverse.at[1], width)
 
+    def panel_arrived(k):
+        @pl.when(me_col == k)
+        def _():
+            panel_local(k).wait()
+
+        @pl.when(me_col != k)
+        def _():
+            panel_copy(k, 1).wait_recv()
+
+    def across_arrived(k, slot):
+        @pl.when(me_row == k)
+        def _():
+            across_local(k, slot).wait()
+
+        @pl.when(me_row != k)
+        def _():
+            across_copy(k, slot, 1).wait_recv()
+
+    total = row_blocks * rows_here
     for k in range(PANELS):
-
-        @pl.when(me_col == k)
-        def _(k=k):
-            panel_local(k).wait()
-
-        @pl.when(me_col != k)
-        def _(k=k):
-            panel_copy(k, 1).wait_recv()
-
-        @pl.when(me_row == k)
-        def _(k=k):
-            across_local(k).wait()
-
-        @pl.when(me_row != k)
-        def _(k=k):
-            across_copy(k, 1).wait_recv()
-
-    left[0] = matmul_t(panel[0], inverse[0])
-    left[1] = matmul_t(panel[1] - matmul_t(left[0], cross[...]), inverse[1])
-    right0 = matmul(inverse[0], across[0])
-    right1 = matmul(inverse[1], across[1] - matmul(cross[...], right0))
-    here = stripe(me_layer)
+        panel_arrived(k)
+    left[0] = matmul_t(panel[0].reshape(total, width), inverse[0])
+    left[1] = matmul_t(panel[1].reshape(total, width) - matmul_t(left[0], cross[...]), inverse[1])
     first0 = jnp.where(me_row == 0, factor[0, here, :], left[0, :rows_here, :])
     first1 = jnp.where(me_row == 0, 0.0, jnp.where(me_row == 1, factor[1, here, :], left[1, :rows_here, :]))
-    updated = share[...] - matmul(left[0], right0) - matmul(left[1], right1)
+
+    def out_copy(slot):
+        return pltpu.make_async_copy(staged.at[slot], out.at[:, 0, :, slot, 0, :], out_sem.at[slot])
+
     for slot in range(col_blocks):
+        for k in range(PANELS):
+            across_arrived(k, slot)
+        share_copy(slot).wait()
+        right0 = matmul(inverse[0], across[0, slot])
+        right1 = matmul(inverse[1], across[1, slot] - matmul(cross[...], right0))
+        updated = share[slot].reshape(total, width) - matmul(left[0], right0) - matmul(left[1], right1)
         number = slot * grid_cols + me_col
-        columns = slice(slot * width, (slot + 1) * width)
-        out[:, columns] = jnp.where(number == 0, left[0], jnp.where(number == 1, left[1], updated[:, columns]))
-        plain = jnp.where(me_row < PANELS, 0.0, updated[:rows_here, columns])
-        out[:rows_here, columns] = jnp.where(number == 0, first0, jnp.where(number == 1, first1, plain))
+        value = jnp.where(number == 0, left[0], jnp.where(number == 1, left[1], updated))
+        staged[slot] = value.reshape(row_blocks, rows_here, width)
+        plain = jnp.where(me_row < PANELS, 0.0, updated[:rows_here])
+        staged[slot, 0] = jnp.where(number == 0, first0, jnp.where(number == 1, first1, plain))
+        out_copy(slot).start()
 
     for b in range(len(BLOCKS)):
 
@@ -239,30 +258,31 @@
 
         @pl.when(me_row == k)
         def _(k=k):
-            for n in range(1, grid_rows):
-                across_copy(k, n).wait_send()
+            for slot in range(col_blocks):
+                for n in range(1, grid_rows):
+                    across_copy(k, slot, n).wait_send()
+    for slot in range(col_blocks):
+        out_copy(slot).wait()
 
 
 def local(sizes, schur_window):
     layers, grid_rows, grid_cols, row_blocks, col_blocks, width = sizes
     rows_here = width // layers
-    held = schur_window.reshape(row_blocks, width, col_blocks * width)
-    share = lax.dynamic_slice_in_dim(held, lax.axis_index("layer") * rows_here, rows_here, 1)
-    share = share.reshape(row_blocks * rows_here, col_blocks * width)
-    top = held[0]
-    vmem = pl.BlockSpec(memory_space=pltpu.VMEM)
+    anywhere = pl.BlockSpec(memory_space=pl.ANY)
     dma = pltpu.SemaphoreType.DMA
     diagonals, peers, half = len(BLOCKS), grid_rows * grid_cols - 1, width // 2
     f32 = jnp.float32
-    result = pl.pallas_call(
+    return pl.pallas_call(
         functools.partial(kernel, sizes),
-        out_shape=jax.ShapeDtypeStruct(share.shape, f32),
-        in_specs=[vmem, vmem],
-        out_specs=vmem,
+        out_shape=jax.ShapeDtypeStruct((row_blocks, 1, rows_here, col_blocks, 1, width), f32),
+        in_specs=[anywhere],
+        out_specs=anywhere,
         scratch_shapes=[
             pltpu.VMEM((diagonals, width, width), f32),
-            pltpu.VMEM((PANELS, width, col_blocks * width), f32),
-            pltpu.VMEM((PANELS, row_blocks * rows_here, width), f32),
+            pltpu.VMEM((PANELS, col_blocks, width, width), f32),
+            pltpu.VMEM((PANELS, row_blocks, rows_here, width), f32),
+            pltpu.VMEM((col_blocks, row_blocks, rows_here, width), f32),
+            pltpu.VMEM((col_blocks, row_blocks, rows_here, width), f32),
             pltpu.VMEM((half, width), f32),
             pltpu.VMEM((PANELS, width, width), f32),
             pltpu.VMEM((PANELS, width, width), f32),
@@ -273,16 +293,17 @@
             dma((diagonals,)),
             dma((diagonals, layers - 1)),
             dma((diagonals, layers - 1)),
-            dma((PANELS, grid_rows - 1)),
-            dma((PANELS,)),
+            dma((PANELS, col_blocks, grid_rows - 1)),
+            dma((PANELS, col_blocks)),
             dma((PANELS, grid_cols - 1)),
             dma((PANELS,)),
-            dma((diagonals + 2 * PANELS,)),
+            dma((diagonals,)),
+            dma((col_blocks,)),
+            dma((col_blocks,)),
         ],
         compiler_params=pltpu.CompilerParams(collective_id=0, has_side_effects=True),
         name="window",
-    )(top, share)
-    return result.reshape(row_blocks, 1, rows_here, col_blocks, 1, width)
+    )(schur_window)
 
 
 def solution(mesh):

time: 84.1 us -> 68.8 us (0.82)
  local copies, waits for them, and re-layouts: 10.6 us -> 2.19 us
  other arithmetic: 7.7 us -> 0 us
  Pallas kernels: 65.5 us -> 66.4 us
    unnamed x1 -> x0, other arithmetic: 7.7 us -> none
    reshape x2 -> x0, local copies, waits for them, and re-layouts: 5.2 us -> none  [the longest x1 2.74 us: local(): held = schur_window.reshape(row_blocks, width, col_blocks * width)]
    slice x1 -> x0, local copies, waits for them, and re-layouts: 2.68 us -> none  [local(): top = held[0]]
    dynamic_slice x1 -> x0, local copies, waits for them, and re-layouts: 1.87 us -> none  [local(): lax.dynamic_slice_in_dim(held, lax.axis_index('layer') * rows_here, rows_...]
    unnamed x1, local copies, waits for them, and re-layouts: 0.83 us -> 2.19 us
    pallas_call x1, Pallas kernels: 65.5 us -> 66.4 us  [local(): pl.pallas_call(functools.partial(kernel, sizes), out_shape=jax.ShapeDtype...]
where the time goes in v2:
time: 68.8 us; the launch traced here: 68.6 us
  Pallas kernels  66.4 us (97%)
  local copies, waits for them, and re-layouts  2.19 us (3%)
    pallas_call x1, Pallas kernels, local(): pl.pallas_call(functools.partial(kernel, sizes), out_shape=jax.ShapeDtype...  66.4 us
    unnamed x1, local copies, waits for them, and re-layouts  2.19 us

profile of v2, /device:TPU:29, one launch (start us, length us, event | category | flops | bytes accessed | tf_op | source)
XLA Modules:
  0.0 68.6 jit_solution(14931301153218082877)
XLA Ops:
  0.0 66.4 %window.2 = f32[4,1,64,2,1,256]{5,4,3,2,1,0:T(1,128)} custom-call(f32[4,1,256,2,1,256]{5,4,3,2,1,0:T(1,128)} %window.3), custom_call_target="tpu_custom_call" | custom-call | tf_op jit(solution)/shard_map/window/pallas_call | solution.py:275
  66.4 2.2 %copy.3 = f32[4,1,64,2,1,256]{5,4,3,2,1,0:T(1,128)} copy(f32[4,1,64,2,1,256]{5,4,3,2,1,0:T(1,128)} %window.2) | data formatting | bytes 1048576

commit v3 on v2

--- a/solution.py
+++ b/solution.py
@@ -27,11 +27,17 @@
     return dot(a, b, 1, 1)
 
 
+def parts(value):
+    high = value.astype(jnp.bfloat16).astype(jnp.float32)
+    mid = (value - high).astype(jnp.bfloat16).astype(jnp.float32)
+    return high, mid, value - high - mid
+
+
 def eliminate(aug, half):
     lane = lax.broadcasted_iota(jnp.int32, (GROUP, half), 1)
     sub = lax.broadcasted_iota(jnp.int32, (GROUP, 2 * half), 0)
 
-    def step(s, carry):
+    def step(start, s, carry):
         first = pl.multiple_of(s * GROUP, GROUP)
         block = aug[pl.ds(first, GROUP), :]
         turned = pltpu.roll(block[:, :half], lax.rem(half - first, half), 1)
@@ -51,11 +57,20 @@
                     entry[k][m] = entry[k][m] - low[k] * low[m]
                 rows[k] = rows[k] - jnp.concatenate([low[k], low[k]], axis=1) * row
         later = jnp.where(lane >= first + GROUP, done[:, :half], 0.0)
-        aug[...] -= dot(later, done, 0, 0)
+        high, mid, low3 = parts(done)
+        high_l, mid_l, low_l = parts(later)
+        lhs = jnp.concatenate([high_l, high_l, mid_l, high_l, low_l, mid_l], axis=0).T
+        rhs = jnp.concatenate([high, mid, high, low3, high, mid], axis=0)
+        aug[start:, :] -= lax.dot_general(
+            lhs[start:], rhs, (((1,), (0,)), ((), ())),
+            precision=lax.Precision.DEFAULT, preferred_element_type=jnp.float32,
+        )
         aug[pl.ds(first, GROUP), :] = done
         return carry
 
-    lax.fori_loop(0, half // GROUP, step, 0)
+    steps = half // GROUP
+    lax.fori_loop(0, steps // 2, functools.partial(step, 0), 0)
+    lax.fori_loop(steps // 2, steps, functools.partial(step, half // 2), 0)
 
 
 def factor_panel(block, aug, factor, inverse, width):

time: 68.8 us -> 62.8 us (0.913)
  Pallas kernels: 66.4 us -> 60.4 us
    pallas_call x1, Pallas kernels: 66.4 us -> 60.4 us  [local(): pl.pallas_call(functools.partial(kernel, sizes), out_shape=jax.ShapeDtype...]
where the time goes in v3:
time: 62.8 us; the launch traced here: 62.7 us
  Pallas kernels  60.4 us (96%)
  local copies, waits for them, and re-layouts  2.19 us (3%)
    pallas_call x1, Pallas kernels, local(): pl.pallas_call(functools.partial(kernel, sizes), out_shape=jax.ShapeDtype...  60.4 us
    unnamed x1, local copies, waits for them, and re-layouts  2.19 us

profile of v3, /device:TPU:29, one launch (start us, length us, event | category | flops | bytes accessed | tf_op | source)
XLA Modules:
  0.0 62.7 jit_solution(5272559981796706157)
XLA Ops:
  0.0 60.4 %window.2 = f32[4,1,64,2,1,256]{5,4,3,2,1,0:T(1,128)} custom-call(f32[4,1,256,2,1,256]{5,4,3,2,1,0:T(1,128)} %window.3), custom_call_target="tpu_custom_call" | custom-call | tf_op jit(solution)/shard_map/window/pallas_call | solution.py:290
  60.5 2.2 %copy.3 = f32[4,1,64,2,1,256]{5,4,3,2,1,0:T(1,128)} copy(f32[4,1,64,2,1,256]{5,4,3,2,1,0:T(1,128)} %window.2) | data formatting | bytes 1048576

commit v4 on v3

--- a/solution.py
+++ b/solution.py
@@ -25,6 +25,17 @@
 
 def matmul_t(a, b):
     return dot(a, b, 1, 1)
+
+
+def update(a, b, rhs):
+    a0, b0 = a.astype(jnp.bfloat16), b.astype(jnp.bfloat16)
+    a1 = (a - a0.astype(jnp.float32)).astype(jnp.bfloat16)
+    b1 = (b - b0.astype(jnp.float32)).astype(jnp.bfloat16)
+
+    def product(x, y):
+        return lax.dot_general(x, y, (((1,), (rhs,)), ((), ())), preferred_element_type=jnp.float32)
+
+    return product(a0, b0) + (product(a0, b1) + product(a1, b0))
 
 
 def parts(value):
@@ -73,7 +84,7 @@
     lax.fori_loop(steps // 2, steps, functools.partial(step, half // 2), 0)
 
 
-def factor_panel(block, aug, factor, inverse, width):
+def factor_panel(block, aug, factor, inverse, width, between):
     half = width // 2
     row = lax.broadcasted_iota(jnp.int32, (half, half), 0)
     col = lax.broadcasted_iota(jnp.int32, (half, half), 1)
@@ -87,6 +98,8 @@
         return jnp.where(row <= col, aug[:, :half], 0.0).T, aug[:, half:]
 
     low1, inv1 = diagonal(block[:half, :half])
+    if between is not None:
+        between()
     factor[:half, :half] = low1
     inverse[:half, :half] = inv1
     factor[:half, half:] = zero
@@ -164,21 +177,34 @@
         return pltpu.make_async_copy(panel_src, panel.at[k], panel_recv.at[k])
 
     owners = [(me_row == i) & (me_col == j) for i, j in BLOCKS]
-    for b in range(len(BLOCKS)):
-
+    def diag_send_out(b):
         @pl.when(owners[b])
-        def _(b=b):
+        def _():
             for n in range(len(grid_peers)):
                 diag_copy(b, n).start()
             diag_local(b).start()
 
+    def diag_pass_on(b):
+        @pl.when(owners[b])
+        def _():
+            diag_local(b).wait()
+
+        @pl.when(jnp.logical_not(owners[b]))
+        def _():
+            diag_copy(b, 0).wait_recv()
+
+        for n in range(1, layers):
+            pass_copy(b, n).start()
+
+    def pass_later():
+        for b in range(1, len(BLOCKS)):
+            diag_pass_on(b)
+
+    diag_send_out(0)
+    diag_pass_on(0)
+    for b in range(1, len(BLOCKS)):
+        diag_send_out(b)
     for k in range(PANELS):
-
-        @pl.when(me_col == k)
-        def _(k=k):
-            for n in range(1, grid_cols):
-                panel_copy(k, n).start()
-            panel_local(k).start()
 
         @pl.when(me_row == k)
         def _(k=k):
@@ -187,30 +213,23 @@
                     across_copy(k, slot, n).start()
                 across_local(k, slot).start()
 
-    for b in range(len(BLOCKS)):
-
-        @pl.when(owners[b])
-        def _(b=b):
-            diag_local(b).wait()
-
-        @pl.when(jnp.logical_not(owners[b]))
-        def _(b=b):
-            diag_copy(b, 0).wait_recv()
-
-        for n in range(1, layers):
-            pass_copy(b, n).start()
+        @pl.when(me_col == k)
+        def _(k=k):
+            for n in range(1, grid_cols):
+                panel_copy(k, n).start()
+            panel_local(k).start()
 
     def diag_arrived(b):
         for n in range(1, layers):
             pass_copy(b, n).wait_recv()
 
     diag_arrived(0)
-    factor_panel(diag.at[0], aug, factor.at[0], inverse.at[0], width)
+    factor_panel(diag.at[0], aug, factor.at[0], inverse.at[0], width, pass_later)
     diag_arrived(1)
     cross[...] = matmul_t(diag[1], inverse[0])
     diag_arrived(2)
     rest[...] = diag[2] - matmul_t(cross[...], cross[...])
-    factor_panel(rest, aug, factor.at[1], inverse.at[1], width)
+    factor_panel(rest, aug, factor.at[1], inverse.at[1], width, None)
 
     def panel_arrived(k):
         @pl.when(me_col == k)
@@ -231,10 +250,11 @@
             across_copy(k, slot, 1).wait_recv()
 
     total = row_blocks * rows_here
+    skipped = rows_here if grid_rows <= PANELS else 0
     for k in range(PANELS):
         panel_arrived(k)
     left[0] = matmul_t(panel[0].reshape(total, width), inverse[0])
-    left[1] = matmul_t(panel[1].reshape(total, width) - matmul_t(left[0], cross[...]), inverse[1])
+    left[1] = matmul_t(panel[1].reshape(total, width) - update(left[0], cross[...], 1), inverse[1])
     first0 = jnp.where(me_row == 0, factor[0, here, :], left[0, :rows_here, :])
     first1 = jnp.where(me_row == 0, 0.0, jnp.where(me_row == 1, factor[1, here, :], left[1, :rows_here, :]))
 
@@ -246,12 +266,14 @@
             across_arrived(k, slot)
         share_copy(slot).wait()
         right0 = matmul(inverse[0], across[0, slot])
-        right1 = matmul(inverse[1], across[1, slot] - matmul(cross[...], right0))
-        updated = share[slot].reshape(total, width) - matmul(left[0], right0) - matmul(left[1], right1)
+        right1 = matmul(inverse[1], across[1, slot] - update(cross[...], right0, 0))
         number = slot * grid_cols + me_col
-        value = jnp.where(number == 0, left[0], jnp.where(number == 1, left[1], updated))
-        staged[slot] = value.reshape(row_blocks, rows_here, width)
-        plain = jnp.where(me_row < PANELS, 0.0, updated[:rows_here])
+        rest_rows = total - skipped
+        updated = share[slot].reshape(total, width)[skipped:]
+        updated -= update(left[0, skipped:, :], right0, 0) + update(left[1, skipped:, :], right1, 0)
+        value = jnp.where(number == 0, left[0, skipped:, :], jnp.where(number == 1, left[1, skipped:, :], updated))
+        staged[slot, skipped // rows_here :] = value.reshape(rest_rows // rows_here, rows_here, width)
+        plain = 0.0 if skipped else jnp.where(me_row < PANELS, 0.0, updated[:rows_here])
         staged[slot, 0] = jnp.where(number == 0, first0, jnp.where(number == 1, first1, plain))
         out_copy(slot).start()
 

time: 62.8 us -> 61.3 us (0.976)
  Pallas kernels: 60.4 us -> 58.9 us
    pallas_call x1, Pallas kernels: 60.4 us -> 58.9 us  [local(): pl.pallas_call(functools.partial(kernel, sizes), out_shape=jax.ShapeDtype...]
where the time goes in v4:
time: 61.3 us; the launch traced here: 61.1 us
  Pallas kernels  58.9 us (96%)
  local copies, waits for them, and re-layouts  2.19 us (4%)
    pallas_call x1, Pallas kernels, local(): pl.pallas_call(functools.partial(kernel, sizes), out_shape=jax.ShapeDtype...  58.9 us
    unnamed x1, local copies, waits for them, and re-layouts  2.19 us

profile of v4, /device:TPU:29, one launch (start us, length us, event | category | flops | bytes accessed | tf_op | source)
XLA Modules:
  0.0 61.1 jit_solution(6923565203766768543)
XLA Ops:
  0.0 58.9 %window.2 = f32[4,1,64,2,1,256]{5,4,3,2,1,0:T(1,128)} custom-call(f32[4,1,256,2,1,256]{5,4,3,2,1,0:T(1,128)} %window.3), custom_call_target="tpu_custom_call" | custom-call | tf_op jit(solution)/shard_map/window/pallas_call | solution.py:312
  58.9 2.2 %copy.3 = f32[4,1,64,2,1,256]{5,4,3,2,1,0:T(1,128)} copy(f32[4,1,64,2,1,256]{5,4,3,2,1,0:T(1,128)} %window.2) | data formatting | bytes 1048576

commit v5 on v4

--- a/solution.py
+++ b/solution.py
@@ -9,7 +9,7 @@
 
 PANELS = 2
 GROUP = 8
-BLOCKS = ((0, 0), (1, 0), (1, 1))
+BLOCKS = ((0, 0, 0, 0), (0, 0, 0, 1), (1, 0, 1, None), (1, 1, 2, None))
 
 
 def dot(a, b, lhs, rhs):
@@ -44,7 +44,7 @@
     return high, mid, value - high - mid
 
 
-def eliminate(aug, half):
+def eliminate(aug, half, midway):
     lane = lax.broadcasted_iota(jnp.int32, (GROUP, half), 1)
     sub = lax.broadcasted_iota(jnp.int32, (GROUP, 2 * half), 0)
 
@@ -81,23 +81,25 @@
 
     steps = half // GROUP
     lax.fori_loop(0, steps // 2, functools.partial(step, 0), 0)
+    if midway is not None:
+        midway()
     lax.fori_loop(steps // 2, steps, functools.partial(step, half // 2), 0)
 
 
-def factor_panel(block, aug, factor, inverse, width, between):
+def factor_panel(block, aug, factor, inverse, width, midway, between):
     half = width // 2
     row = lax.broadcasted_iota(jnp.int32, (half, half), 0)
     col = lax.broadcasted_iota(jnp.int32, (half, half), 1)
     eye = jnp.where(row == col, 1.0, 0.0).astype(jnp.float32)
     zero = jnp.zeros((half, half), jnp.float32)
 
-    def diagonal(value):
+    def diagonal(value, midway):
         aug[:, :half] = value
         aug[:, half:] = eye
-        eliminate(aug, half)
+        eliminate(aug, half, midway)
         return jnp.where(row <= col, aug[:, :half], 0.0).T, aug[:, half:]
 
-    low1, inv1 = diagonal(block[:half, :half])
+    low1, inv1 = diagonal(block[:half, :half], midway)
     if between is not None:
         between()
     factor[:half, :half] = low1
@@ -106,7 +108,7 @@
     inverse[:half, half:] = zero
     below = matmul_t(block[half:, :half], inv1)
     factor[half:, :half] = below
-    low2, inv2 = diagonal(block[half:, half:] - matmul_t(below, below))
+    low2, inv2 = diagonal(block[half:, half:] - matmul_t(below, below), None)
     factor[half:, half:] = low2
     inverse[half:, half:] = inv2
     inverse[half:, :half] = -matmul(inv2, matmul(below, inverse[:half, :half]))
@@ -147,16 +149,24 @@
         share_copy(slot).start()
     pl.semaphore_wait(barrier, len(grid_peers) + layers - 1)
 
-    diag_src = window.at[0, 0, here, 0, 0, :]
+    def columns(b):
+        side = BLOCKS[b][3]
+        return pl.ds(0, width) if side is None else pl.ds(side * (width // 2), width // 2)
+
+    def diag_src(b):
+        return window.at[0, 0, here, 0, 0, columns(b)]
+
+    def diag_dst(b):
+        return diag.at[BLOCKS[b][2], here, columns(b)]
 
     def diag_copy(b, n):
-        return remote(diag_src, diag.at[b, here, :], diag_send.at[b, n], diag_recv.at[b], at(0, *grid_peers[n]))
+        return remote(diag_src(b), diag_dst(b), diag_send.at[b, n], diag_recv.at[b], at(0, *grid_peers[n]))
 
     def diag_local(b):
-        return pltpu.make_async_copy(diag_src, diag.at[b, here, :], local_sem.at[b])
+        return pltpu.make_async_copy(diag_src(b), diag_dst(b), local_sem.at[b])
 
     def pass_copy(b, n):
-        part = diag.at[b, here, :]
+        part = diag_dst(b)
         return remote(part, part, pass_send.at[b, n - 1], pass_recv.at[b, n - 1], at(n, 0, 0))
 
     def across_copy(k, slot, n):
@@ -176,7 +186,7 @@
     def panel_local(k):
         return pltpu.make_async_copy(panel_src, panel.at[k], panel_recv.at[k])
 
-    owners = [(me_row == i) & (me_col == j) for i, j in BLOCKS]
+    owners = [(me_row == i) & (me_col == j) for i, j, _, _ in BLOCKS]
     def diag_send_out(b):
         @pl.when(owners[b])
         def _():
@@ -196,9 +206,13 @@
         for n in range(1, layers):
             pass_copy(b, n).start()
 
-    def pass_later():
-        for b in range(1, len(BLOCKS)):
+    def midway():
+        diag_pass_on(1)
+
+    def between():
+        for b in range(2, len(BLOCKS)):
             diag_pass_on(b)
+        diag_arrived(1)
 
     diag_send_out(0)
     diag_pass_on(0)
@@ -224,12 +238,12 @@
             pass_copy(b, n).wait_recv()
 
     diag_arrived(0)
-    factor_panel(diag.at[0], aug, factor.at[0], inverse.at[0], width, pass_later)
-    diag_arrived(1)
+    factor_panel(diag.at[0], aug, factor.at[0], inverse.at[0], width, midway, between)
+    diag_arrived(2)
     cross[...] = matmul_t(diag[1], inverse[0])
-    diag_arrived(2)
+    diag_arrived(3)
     rest[...] = diag[2] - matmul_t(cross[...], cross[...])
-    factor_panel(rest, aug, factor.at[1], inverse.at[1], width, None)
+    factor_panel(rest, aug, factor.at[1], inverse.at[1], width, None, None)
 
     def panel_arrived(k):
         @pl.when(me_col == k)
@@ -307,7 +321,7 @@
     rows_here = width // layers
     anywhere = pl.BlockSpec(memory_space=pl.ANY)
     dma = pltpu.SemaphoreType.DMA
-    diagonals, peers, half = len(BLOCKS), grid_rows * grid_cols - 1, width // 2
+    sends, diagonals, peers, half = len(BLOCKS), len({b[2] for b in BLOCKS}), grid_rows * grid_cols - 1, width // 2
     f32 = jnp.float32
     return pl.pallas_call(
         functools.partial(kernel, sizes),
@@ -326,15 +340,15 @@
             pltpu.VMEM((width, width), f32),
             pltpu.VMEM((width, width), f32),
             pltpu.VMEM((PANELS, row_blocks * rows_here, width), f32),
-            dma((diagonals, peers)),
-            dma((diagonals,)),
-            dma((diagonals, layers - 1)),
-            dma((diagonals, layers - 1)),
+            dma((sends, peers)),
+            dma((sends,)),
+            dma((sends, layers - 1)),
+            dma((sends, layers - 1)),
             dma((PANELS, col_blocks, grid_rows - 1)),
             dma((PANELS, col_blocks)),
             dma((PANELS, grid_cols - 1)),
             dma((PANELS,)),
-            dma((diagonals,)),
+            dma((sends,)),
             dma((col_blocks,)),
             dma((col_blocks,)),
         ],

time: 61.3 us -> 57.6 us (0.940)
  the two profiles are of different devices: /device:TPU:29 before, /device:TPU:26 now
where the time goes in v5:
time: 57.6 us; the launch traced here: 57.4 us
  Pallas kernels  55.2 us (96%)
  local copies, waits for them, and re-layouts  2.19 us (4%)
    pallas_call x1, Pallas kernels, local(): pl.pallas_call(functools.partial(kernel, sizes), out_shape=jax.ShapeDtype...  55.2 us
    unnamed x1, local copies, waits for them, and re-layouts  2.19 us

profile of v5, /device:TPU:26, one launch (start us, length us, event | category | flops | bytes accessed | tf_op | source)
XLA Modules:
  0.0 57.4 jit_solution(12054795394129356611)
XLA Ops:
  0.0 55.2 %window.2 = f32[4,1,64,2,1,256]{5,4,3,2,1,0:T(1,128)} custom-call(f32[4,1,256,2,1,256]{5,4,3,2,1,0:T(1,128)} %window.3), custom_call_target="tpu_custom_call" | custom-call | tf_op jit(solution)/shard_map/window/pallas_call | solution.py:326
  55.2 2.2 %copy.3 = f32[4,1,64,2,1,256]{5,4,3,2,1,0:T(1,128)} copy(f32[4,1,64,2,1,256]{5,4,3,2,1,0:T(1,128)} %window.2) | data formatting | bytes 1048576

commit v6 on v5

--- a/solution.py
+++ b/solution.py
@@ -140,6 +140,7 @@
         return pltpu.make_async_copy(window.at[:, 0, here, slot, 0, :], share.at[slot], share_sem.at[slot])
 
     grid_peers = [(row, col) for row in range(grid_rows) for col in range(grid_cols) if row or col]
+    grid_peers.sort(key=lambda peer: -sum(peer))
     barrier = pltpu.get_barrier_semaphore()
     for row, col in grid_peers:
         pl.semaphore_signal(barrier, inc=1, device_id=at(0, row, col), device_id_type=pl.DeviceIdType.MESH)

time: 57.6 us -> 56.9 us (0.988)
  the two profiles are of different devices: /device:TPU:26 before, /device:TPU:9 now
where the time goes in v6:
time: 56.9 us; the launch traced here: 56.6 us
  Pallas kernels  54.4 us (96%)
  local copies, waits for them, and re-layouts  2.19 us (4%)
    pallas_call x1, Pallas kernels, local(): pl.pallas_call(functools.partial(kernel, sizes), out_shape=jax.ShapeDtype...  54.4 us
    unnamed x1, local copies, waits for them, and re-layouts  2.19 us

profile of v6, /device:TPU:9, one launch (start us, length us, event | category | flops | bytes accessed | tf_op | source)
XLA Modules:
  0.0 56.6 jit_solution(12738321517056552784)
XLA Ops:
  0.0 54.4 %window.2 = f32[4,1,64,2,1,256]{5,4,3,2,1,0:T(1,128)} custom-call(f32[4,1,256,2,1,256]{5,4,3,2,1,0:T(1,128)} %window.3), custom_call_target="tpu_custom_call" | custom-call | tf_op jit(solution)/shard_map/window/pallas_call | solution.py:327
  54.4 2.2 %copy.3 = f32[4,1,64,2,1,256]{5,4,3,2,1,0:T(1,128)} copy(f32[4,1,64,2,1,256]{5,4,3,2,1,0:T(1,128)} %window.2) | data formatting | bytes 1048576
